TPU v7x, 32 devices: a whole 2x2x4 slice. The times are simulated.
32 devices in a mesh: ra: 4 (over x, core), rb: 8 (over z, y).
Axes of the slice: x: 2, y: 2, z: 4, core: 2. Of those that a mesh axis runs over, the one named last changes fastest.
Arguments:
- amplitude: bfloat16 [2, 512, 512, 256], P(None, 'ra', 'rb'), may hold values from -6 to 6
- coupling: bfloat16 [6, 256, 256], replicated, may hold values from -0.5 to 0.5
- pattern: int32 [6, 4, 4], replicated, may hold values 0 or 1
- radial: float32 [6, 512, 512], P(None, 'ra', 'rb'), may hold values from -2.4 to 2.4
- first_prop: bfloat16 [2, 512, 512], replicated, may hold values from -0.1875 to 0.1875
- second_prop: bfloat16 [2, 512, 512], replicated, may hold values from -0.1875 to 0.1875
Outputs:
- evolved: bfloat16 [2, 512, 512, 256], P(None, 'ra', 'rb')
All inputs are finite; a program needn't handle non-finite values.
Results may differ from a plain program's by a relative error of at most 0.0095.
Values may be sent and summed in bfloat16 or wider, within the bound.
A program may use at most 128 MiB of HBM per device.

v0:
```python
import jax
import jax.numpy as jnp
from jax import lax
from jax.sharding import PartitionSpec as P

KTERMS = 6
STEPS = 2


def complex_rows(matrix, piece):
    form = "ac,cqw->aqw"
    real_part = jnp.einsum(
        form, matrix[0], piece[0], preferred_element_type=jnp.float32
    ) - jnp.einsum(form, matrix[1], piece[1], preferred_element_type=jnp.float32)
    imag_part = jnp.einsum(
        form, matrix[0], piece[1], preferred_element_type=jnp.float32
    ) + jnp.einsum(form, matrix[1], piece[0], preferred_element_type=jnp.float32)
    return jnp.stack([real_part, imag_part]).astype(jnp.bfloat16)


def on_device(amplitude, coupling, pattern, radial, first_prop, second_prop):
    first_rows, second_rows, channels = (amplitude.shape[1], amplitude.shape[2], amplitude.shape[3])
    cells = first_rows * second_rows
    count = pattern.shape[1]
    block_size = channels // count
    groups_a = lax.axis_size("ra")
    groups_b = lax.axis_size("rb")
    width_a = channels // groups_a
    width_b = channels // groups_b
    spread = jnp.broadcast_to(
        pattern[:, :, None, :, None], (KTERMS, count, block_size, count, block_size)
    )
    block_mask = spread.reshape(KTERMS, channels, channels).astype(jnp.bfloat16)
    weights = coupling * block_mask
    radial_cells = radial.reshape(KTERMS, cells).T
    for sweep in range(STEPS):
        flat = amplitude.reshape(2 * cells, channels)
        applied = jnp.einsum("mj,kij->mki", flat, weights, preferred_element_type=jnp.float32)
        applied = applied.reshape(2, cells, KTERMS, channels)
        coupled = jnp.sum(applied * radial_cells[None, :, :, None], axis=2)
        wide = amplitude.reshape(2, cells, channels).astype(jnp.float32)
        kicked = jnp.stack([wide[0] + coupled[1], wide[1] - coupled[0]]).astype(jnp.bfloat16)
        grouped = kicked.reshape(2, first_rows, second_rows, groups_a, width_a)
        grouped = grouped.transpose(0, 1, 3, 2, 4).reshape(
            2, first_rows, groups_a, second_rows * width_a
        )
        half = complex_rows(
            first_prop, lax.all_to_all(grouped, "ra", split_axis=2, concat_axis=1, tiled=True)
        )
        restored = lax.all_to_all(half, "ra", split_axis=1, concat_axis=2, tiled=True)
        restored = restored.reshape(2, first_rows, groups_a, second_rows, width_a)
        restored = restored.transpose(0, 1, 3, 2, 4).reshape(
            2, first_rows, second_rows, groups_b, width_b
        )
        regrouped = restored.transpose(0, 2, 3, 1, 4).reshape(
            2, second_rows, groups_b, first_rows * width_b
        )
        moved = complex_rows(
            second_prop, lax.all_to_all(regrouped, "rb", split_axis=2, concat_axis=1, tiled=True)
        )
        settled = lax.all_to_all(moved, "rb", split_axis=1, concat_axis=2, tiled=True)
        settled = settled.reshape(2, second_rows, groups_b, first_rows, width_b)
        amplitude = settled.transpose(0, 3, 1, 2, 4).reshape(2, first_rows, second_rows, channels)
    return amplitude


def solution(mesh):
    return jax.shard_map(
        on_device,
        mesh=mesh,
        in_specs=(P(None, "ra", "rb", None), P(), P(), P(None, "ra", "rb"), P(), P()),
        out_specs=P(None, "ra", "rb", None),
        check_vma=False,
    )
```

profile of v0, /device:TPU:0, one launch (start us, length us, event | category | flops | bytes accessed | tf_op | source)
XLA Modules:
  0.0 1957.4 jit_solution(6471844927591130573)
XLA Ops:
  34.3 23.9 %fusion = f32[16384,256]{0,1:T(8,128)} fusion(f32[16384,6]{0,1:T(8,128)S(1)} %bitcast.242, bf16[16384,256,1]{1,0,2:T(8,128)(2,1)} %bitcast.213, bf16[6,256,256]{2,1,0:T(8,128)(2,1)S(1)} %copy-done.8, bf16[6,256,256]{2,1,0:T(8,128)(2,1)S(1)} %convert_element_type.56), kind=kOutput, calls=%fused_computation.1 | convolution fusion | flops 12931432448 | bytes 27131904 | tf_op jit(solution)/shard_map/mj,kij->mki/dot_general | solution.py:38
  113.1 18.7 copy.168
  131.8 101.7 %all_to_all.120 = bf16[2,128,4,4096]{1,3,0,2:T(8,128)(2,1)} all-to-all(bf16[2,128,4,4096]{1,3,0,2:T(8,128)(2,1)} %bitcast.206), channel_id=1, replica_groups=mesh['ra'=4,'rb'=8] {'ra'}, dimensions={2} | all-to-all | bytes 16777216 | tf_op jit(solution)/shard_map/all_to_all | solution.py:48
  271.1 21.5 %copy.137 = bf16[2,512,1,4096]{3,0,2,1:T(2,128)(2,1)} copy(bf16[2,512,1,4096]{1,3,2,0:T(8,128)(2,1)} %pad_maximum_fusion) | data formatting | bytes 16777216 | tf_op jit(solution)/shard_map/stack | solution.py:18
  292.6 100.7 %all_to_all.121 = bf16[2,512,1,4096]{3,0,2,1:T(2,128)(2,1)} all-to-all(bf16[2,512,1,4096]{3,0,2,1:T(2,128)(2,1)} %copy.137), channel_id=1, replica_groups=mesh['ra'=4,'rb'=8] {'ra'}, dimensions={1} | all-to-all | bytes 16777216 | tf_op jit(solution)/shard_map/all_to_all | solution.py:50
  427.8 29.1 %copy.141 = bf16[2,64,8,128,32]{1,4,3,2,0:T(8,128)(2,1)} copy(bf16[2,64,8,128,32]{3,4,2,1,0:T(8,128)(2,1)} %bitcast.207) | data formatting | bytes 16777216 | tf_op jit(solution)/shard_map/transpose | solution.py:55
  457.0 15.8 copy.142
  472.8 190.0 %all_to_all.122 = bf16[2,64,8,4096]{3,1,0,2:T(8,128)(2,1)} all-to-all(bf16[2,64,8,4096]{3,1,0,2:T(8,128)(2,1)} %copy.142), channel_id=1, replica_groups=mesh['ra'=4,'rb'=8] {'rb'}, dimensions={2} | all-to-all | bytes 16777216 | tf_op jit(solution)/shard_map/all_to_all | solution.py:59
  696.3 21.5 %copy.144 = bf16[2,512,1,4096]{3,0,2,1:T(2,128)(2,1)} copy(bf16[2,512,1,4096]{1,3,2,0:T(8,128)(2,1)} %pad_maximum_fusion.1) | data formatting | bytes 16777216 | tf_op jit(solution)/shard_map/stack | solution.py:18
  723.3 182.0 %all-to-all-done.3 = bf16[2,512,1,4096]{3,0,2,1:T(2,128)(2,1)} async-done(((bf16[2,512,1,4096]{3,0,2,1:T(2,128)(2,1)}), bf16[2,512,1,4096]{3,0,2,1:T(2,128)(2,1)}, u32[]{:S(2)}, u32[]{:S(2)}) %all-to-all-start.3) | async-done | bytes 8388640 | tf_op jit(solution)/shard_map/all_to_all | solution.py:61
  918.1 15.5 copy.146
  933.7 17.5 copy.147
  951.2 22.5 %reshape_reshape.4 = bf16[2,8192,256]{1,2,0:T(8,128)(2,1)} reshape(bf16[2,128,64,8,32]{2,1,4,3,0:T(8,128)(2,1)} %copy.147) | data formatting | bytes 16777216 | tf_op jit(solution)/shard_map/reshape;reshape | solution.py:41
  985.7 33.8 %multiply_reduce_fusion = f32[2,8192,256]{2,1,0:T(8,128)} fusion(f32[8192,6]{0,1:T(8,128)S(1)} %bitcast.241, bf16[2,8192,256]{1,2,0:T(8,128)(2,1)} %reshape_reshape.4, bf16[6,256,256,1]{2,1,0,3:T(8,128)(2,1)S(1)} %fusion.84), kind=kOutput, calls=%fused_computation.2 | convolution fusion | flops 12931039232 | bytes 26148864 | tf_op jit(solution)/shard_map/mj,kij->mki/dot_general | solution.py:38
  1097.8 18.7 copy.171
  1116.5 100.8 %all_to_all.123 = bf16[2,128,4,4096]{1,3,0,2:T(8,128)(2,1)} all-to-all(bf16[2,128,4,4096]{1,3,0,2:T(8,128)(2,1)} %bitcast.209), channel_id=1, replica_groups=mesh['ra'=4,'rb'=8] {'ra'}, dimensions={2} | all-to-all | bytes 16777216 | tf_op jit(solution)/shard_map/all_to_all | solution.py:48
  1254.8 21.5 %copy.155 = bf16[2,512,1,4096]{3,0,2,1:T(2,128)(2,1)} copy(bf16[2,512,1,4096]{1,3,2,0:T(8,128)(2,1)} %pad_maximum_fusion.2) | data formatting | bytes 16777216 | tf_op jit(solution)/shard_map/stack | solution.py:18
  1276.3 100.9 %all_to_all.124 = bf16[2,512,1,4096]{3,0,2,1:T(2,128)(2,1)} all-to-all(bf16[2,512,1,4096]{3,0,2,1:T(2,128)(2,1)} %copy.155), channel_id=1, replica_groups=mesh['ra'=4,'rb'=8] {'ra'}, dimensions={1} | all-to-all | bytes 16777216 | tf_op jit(solution)/shard_map/all_to_all | solution.py:50
  1411.8 29.1 %copy.159 = bf16[2,64,8,128,32]{1,4,3,2,0:T(8,128)(2,1)} copy(bf16[2,64,8,128,32]{3,4,2,1,0:T(8,128)(2,1)} %bitcast.210) | data formatting | bytes 16777216 | tf_op jit(solution)/shard_map/transpose | solution.py:55
  1440.9 15.8 copy.160
  1456.7 188.9 %all_to_all.125 = bf16[2,64,8,4096]{3,1,0,2:T(8,128)(2,1)} all-to-all(bf16[2,64,8,4096]{3,1,0,2:T(8,128)(2,1)} %copy.160), channel_id=1, replica_groups=mesh['ra'=4,'rb'=8] {'rb'}, dimensions={2} | all-to-all | bytes 16777216 | tf_op jit(solution)/shard_map/all_to_all | solution.py:59
  1679.0 21.5 %copy.162 = bf16[2,512,1,4096]{3,0,2,1:T(2,128)(2,1)} copy(bf16[2,512,1,4096]{1,3,2,0:T(8,128)(2,1)} %pad_maximum_fusion.3) | data formatting | bytes 16777216 | tf_op jit(solution)/shard_map/stack | solution.py:18
  1700.6 188.5 %all_to_all.126 = bf16[2,512,1,4096]{3,0,2,1:T(2,128)(2,1)} all-to-all(bf16[2,512,1,4096]{3,0,2,1:T(2,128)(2,1)} %copy.162), channel_id=1, replica_groups=mesh['ra'=4,'rb'=8] {'rb'}, dimensions={1} | all-to-all | bytes 16777216 | tf_op jit(solution)/shard_map/all_to_all | solution.py:61
  1917.4 27.6 %copy.165 = bf16[2,128,64,8,32]{1,4,3,2,0:T(8,128)(2,1)} copy(bf16[2,128,64,8,32]{2,4,1,3,0:T(8,128)(2,1)} %bitcast.204) | data formatting | bytes 16777216 | tf_op jit(solution)/shard_map/transpose | solution.py:63
  (83 shorter events, 449.2 us)
Async XLA Ops:
  2.1 0.7 copy-start.6
  4.5 29.8 %copy-start.4 = (bf16[6,256,256]{2,1,0:T(8,128)(2,1)}, bf16[6,256,256]{2,1,0:T(8,128)(2,1)S(1)}, u32[]{:S(2)}) copy-start(bf16[6,256,256]{2,1,0:T(8,128)(2,1)S(1)} %convert_element_type.56) | copy-start | bytes 2359300
  25.3 9.0 copy-start.8
  245.5 3.9 copy-start
  670.7 3.9 copy-start.2
  717.7 5.5 copy-start.5
  717.7 5.5 copy-start.9
  717.7 187.6 %all-to-all-start.3 = ((bf16[2,512,1,4096]{3,0,2,1:T(2,128)(2,1)}), bf16[2,512,1,4096]{3,0,2,1:T(2,128)(2,1)}, u32[]{:S(2)}, u32[]{:S(2)}) async-start(bf16[2,512,1,4096]{3,0,2,1:T(2,128)(2,1)} %copy.144), calls=%async_computation.3 | async-start | bytes 16777216 | tf_op jit(solution)/shard_map/all_to_all | solution.py:61
  973.7 12.0 copy-start.7
  1229.2 3.9 copy-start.1
  1653.5 3.9 copy-start.3
where the time goes:
time: 1980 us; the launch traced here: 1960 us
  blocking collectives  972 us (49%)
  local copies, waits for them, and re-layouts  583 us (29%)
  waiting for transfers between devices  182 us (9%)
  matrix products  114 us (6%)
  other arithmetic  102 us (5%)
    all_to_all x2, blocking collectives, on_device(): lax.all_to_all(regrouped, 'rb', split_axis=2, concat_axis=1, tiled=True)  379 us
    all_to_all x2, blocking collectives, on_device(): lax.all_to_all(grouped, 'ra', split_axis=2, concat_axis=1, tiled=True)  203 us
    all_to_all x2, blocking collectives, on_device(): lax.all_to_all(half, 'ra', split_axis=1, concat_axis=2, tiled=True)  202 us
    all_to_all x1, blocking collectives, on_device(): lax.all_to_all(moved, 'rb', split_axis=1, concat_axis=2, tiled=True)  189 us
    all_to_all x1, waiting for transfers between devices, on_device(): lax.all_to_all(moved, 'rb', split_axis=1, concat_axis=2, tiled=True)  182 us
    another operation x4, local copies, waits for them, and re-layouts, complex_rows(): return jnp.stack([real_part, imag_part]).astype(jnp.bfloat16)  86 us
    transpose x2, local copies, waits for them, and re-layouts, on_device(): restored.transpose(0, 2, 3, 1, 4)  58.3 us
    dot_general x2, matrix products, on_device(): jnp.einsum('mj,kij->mki', flat, weights, preferred_element_type=jnp.float32)  57.7 us
  transfers between devices with their start and end apart: 1, of which 1 were waited for; matrix products, arithmetic and copies ran while one was open for 0% of the time, Pallas kernels for 0%

commit v1 on v0

--- a/solution.py
+++ b/solution.py
@@ -47,7 +47,10 @@
         half = complex_rows(
             first_prop, lax.all_to_all(grouped, "ra", split_axis=2, concat_axis=1, tiled=True)
         )
-        restored = lax.all_to_all(half, "ra", split_axis=1, concat_axis=2, tiled=True)
+        feed_layers_all_now = lambda target: jnp.concatenate(
+            lax.all_to_all(jnp.stack(jnp.split(target, lax.axis_size("ra"), 1), 0), "ra", 0, 0), 2
+        )
+        restored = feed_layers_all_now(half)
         restored = restored.reshape(2, first_rows, groups_a, second_rows, width_a)
         restored = restored.transpose(0, 1, 3, 2, 4).reshape(
             2, first_rows, second_rows, groups_b, width_b

time: 1980 us -> 1900 us (0.960)
  local copies, waits for them, and re-layouts: 583 us -> 501 us
    all_to_all x4 -> x0, local copies, waits for them, and re-layouts: 49.5 us -> none  [on_device(): lax.all_to_all(half, 'ra', split_axis=1, concat_axis=2, tiled=True)]
    another operation x4 -> x2, local copies, waits for them, and re-layouts: 86 us -> 43 us  [complex_rows(): return jnp.stack([real_part, imag_part]).astype(jnp.bfloat16)]
    another operation x2 -> x6, local copies, waits for them, and re-layouts: 12.6 us -> 38.9 us  [the longest x2 19.6 us: on_device(): restored = restored.reshape(2, first_rows, groups_a, second_rows, width_a)]
    another operation x2 -> x6, other arithmetic: 30.4 us -> 44.9 us
where the time goes in v1:
time: 1900 us; the launch traced here: 1890 us
  blocking collectives  963 us (51%)
  local copies, waits for them, and re-layouts  501 us (26%)
  waiting for transfers between devices  182 us (10%)
  matrix products  120 us (6%)
  other arithmetic  114 us (6%)
    all_to_all x2, blocking collectives, on_device(): lax.all_to_all(regrouped, 'rb', split_axis=2, concat_axis=1, tiled=True)  379 us
    all_to_all x2, blocking collectives, on_device(): lax.all_to_all(grouped, 'ra', split_axis=2, concat_axis=1, tiled=True)  202 us
    all_to_all x2, blocking collectives, on_device(): lax.all_to_all(jnp.stack(jnp.split(target, lax.axis_size('ra'), 1), 0), '...  194 us
    all_to_all x1, blocking collectives, on_device(): lax.all_to_all(moved, 'rb', split_axis=1, concat_axis=2, tiled=True)  189 us
    all_to_all x1, waiting for transfers between devices, on_device(): lax.all_to_all(moved, 'rb', split_axis=1, concat_axis=2, tiled=True)  182 us
    transpose x2, local copies, waits for them, and re-layouts, on_device(): restored.transpose(0, 2, 3, 1, 4)  58.3 us
    dot_general x2, matrix products, on_device(): jnp.einsum('mj,kij->mki', flat, weights, preferred_element_type=jnp.float32)  57.7 us
    all_to_all x4, local copies, waits for them, and re-layouts, on_device(): lax.all_to_all(moved, 'rb', split_axis=1, concat_axis=2, tiled=True)  56.8 us
  transfers between devices with their start and end apart: 1, of which 1 were waited for; matrix products, arithmetic and copies ran while one was open for 0% of the time, Pallas kernels for 0%

profile of v1, /device:TPU:0, one launch (start us, length us, event | category | flops | bytes accessed | tf_op | source)
XLA Modules:
  0.0 1885.4 jit_solution(17733266962812431367)
XLA Ops:
  34.3 23.9 %fusion = f32[16384,256]{0,1:T(8,128)} fusion(f32[16384,6]{0,1:T(8,128)S(1)} %bitcast.262, bf16[16384,256,1]{1,0,2:T(8,128)(2,1)} %bitcast.235, bf16[6,256,256]{2,1,0:T(8,128)(2,1)S(1)} %copy-done.10, bf16[6,256,256]{2,1,0:T(8,128)(2,1)S(1)} %convert_element_type.56), kind=kOutput, calls=%fused_computation.1 | convolution fusion | flops 12931432448 | bytes 27131904 | tf_op jit(solution)/shard_map/mj,kij->mki/dot_general | solution.py:38
  113.1 18.7 copy.153
  131.9 101.5 %all_to_all.100 = bf16[2,128,4,4096]{1,3,0,2:T(8,128)(2,1)} all-to-all(bf16[2,128,4,4096]{1,3,0,2:T(8,128)(2,1)} %bitcast.228), channel_id=1, replica_groups=mesh['ra'=4,'rb'=8] {'ra'}, dimensions={2} | all-to-all | bytes 16777216 | tf_op jit(solution)/shard_map/all_to_all | solution.py:48
  290.7 96.9 %all_to_all.101 = bf16[4,2,128,1,4096]{2,4,1,3,0:T(8,128)(2,1)} all-to-all(bf16[4,2,128,1,4096]{2,4,1,3,0:T(8,128)(2,1)S(1)} %pad_maximum_fusion.2), channel_id=1, replica_groups=mesh['ra'=4,'rb'=8] {'ra'}, dimensions={0} | all-to-all | bytes 16777216 | tf_op jit(solution)/shard_map/all_to_all | solution.py:51
  397.4 29.2 %copy.126 = bf16[2,64,8,128,32]{1,4,3,2,0:T(8,128)(2,1)} copy(bf16[2,64,8,128,32]{3,4,2,1,0:T(8,128)(2,1)} %bitcast.229) | data formatting | bytes 16777216 | tf_op jit(solution)/shard_map/transpose | solution.py:58
  426.5 15.8 copy.127
  442.3 189.8 %all_to_all.102 = bf16[2,64,8,4096]{3,1,0,2:T(8,128)(2,1)} all-to-all(bf16[2,64,8,4096]{3,1,0,2:T(8,128)(2,1)} %copy.127), channel_id=1, replica_groups=mesh['ra'=4,'rb'=8] {'rb'}, dimensions={2} | all-to-all | bytes 16777216 | tf_op jit(solution)/shard_map/all_to_all | solution.py:62
  665.6 21.5 %copy.129 = bf16[2,512,1,4096]{3,0,2,1:T(2,128)(2,1)} copy(bf16[2,512,1,4096]{1,3,2,0:T(8,128)(2,1)} %pad_maximum_fusion.3) | data formatting | bytes 16777216 | tf_op jit(solution)/shard_map/stack | solution.py:18
  692.7 182.0 %all-to-all-done.3 = bf16[2,512,1,4096]{3,0,2,1:T(2,128)(2,1)} async-done(((bf16[2,512,1,4096]{3,0,2,1:T(2,128)(2,1)}), bf16[2,512,1,4096]{3,0,2,1:T(2,128)(2,1)}, u32[]{:S(2)}, u32[]{:S(2)}) %all-to-all-start.3) | async-done | bytes 8388640 | tf_op jit(solution)/shard_map/all_to_all | solution.py:64
  887.6 15.6 copy.131
  903.1 17.5 copy.132
  920.6 22.5 %reshape_reshape.11 = bf16[2,8192,256]{1,2,0:T(8,128)(2,1)} reshape(bf16[2,128,64,8,32]{2,1,4,3,0:T(8,128)(2,1)} %copy.132) | data formatting | bytes 16777216 | tf_op jit(solution)/shard_map/reshape;reshape | solution.py:41
  955.2 33.8 %multiply_reduce_fusion = f32[2,8192,256]{2,1,0:T(8,128)} fusion(f32[8192,6]{0,1:T(8,128)S(1)} %bitcast.261, bf16[2,8192,256]{1,2,0:T(8,128)(2,1)} %reshape_reshape.11, bf16[6,256,256,1]{2,1,0,3:T(8,128)(2,1)S(1)} %fusion.90), kind=kOutput, calls=%fused_computation.2 | convolution fusion | flops 12931039232 | bytes 26148864 | tf_op jit(solution)/shard_map/mj,kij->mki/dot_general | solution.py:38
  999.5 15.3 fusion.4
  1067.4 18.7 copy.156
  1086.2 101.0 %all_to_all.103 = bf16[2,128,4,4096]{1,3,0,2:T(8,128)(2,1)} all-to-all(bf16[2,128,4,4096]{1,3,0,2:T(8,128)(2,1)} %bitcast.231), channel_id=1, replica_groups=mesh['ra'=4,'rb'=8] {'ra'}, dimensions={2} | all-to-all | bytes 16777216 | tf_op jit(solution)/shard_map/all_to_all | solution.py:48
  1233.1 96.9 %all_to_all.104 = bf16[4,2,128,1,4096]{2,4,1,3,0:T(8,128)(2,1)} all-to-all(bf16[4,2,128,1,4096]{2,4,1,3,0:T(8,128)(2,1)S(1)} %pad_maximum_fusion.4), channel_id=1, replica_groups=mesh['ra'=4,'rb'=8] {'ra'}, dimensions={0} | all-to-all | bytes 16777216 | tf_op jit(solution)/shard_map/all_to_all | solution.py:51
  1339.8 29.2 %copy.144 = bf16[2,64,8,128,32]{1,4,3,2,0:T(8,128)(2,1)} copy(bf16[2,64,8,128,32]{3,4,2,1,0:T(8,128)(2,1)} %bitcast.232) | data formatting | bytes 16777216 | tf_op jit(solution)/shard_map/transpose | solution.py:58
  1368.9 15.8 copy.145
  1384.7 188.7 %all_to_all.105 = bf16[2,64,8,4096]{3,1,0,2:T(8,128)(2,1)} all-to-all(bf16[2,64,8,4096]{3,1,0,2:T(8,128)(2,1)} %copy.145), channel_id=1, replica_groups=mesh['ra'=4,'rb'=8] {'rb'}, dimensions={2} | all-to-all | bytes 16777216 | tf_op jit(solution)/shard_map/all_to_all | solution.py:62
  1606.9 21.5 %copy.147 = bf16[2,512,1,4096]{3,0,2,1:T(2,128)(2,1)} copy(bf16[2,512,1,4096]{1,3,2,0:T(8,128)(2,1)} %pad_maximum_fusion.5) | data formatting | bytes 16777216 | tf_op jit(solution)/shard_map/stack | solution.py:18
  1628.4 188.5 %all_to_all.106 = bf16[2,512,1,4096]{3,0,2,1:T(2,128)(2,1)} all-to-all(bf16[2,512,1,4096]{3,0,2,1:T(2,128)(2,1)} %copy.147), channel_id=1, replica_groups=mesh['ra'=4,'rb'=8] {'rb'}, dimensions={1} | all-to-all | bytes 16777216 | tf_op jit(solution)/shard_map/all_to_all | solution.py:64
  1829.8 15.6 copy.149
  1845.3 27.6 %copy.150 = bf16[2,128,64,8,32]{1,4,3,2,0:T(8,128)(2,1)} copy(bf16[2,128,64,8,32]{2,4,1,3,0:T(8,128)(2,1)} %bitcast.226) | data formatting | bytes 16777216 | tf_op jit(solution)/shard_map/transpose | solution.py:66
  (87 shorter events, 397.2 us)
Async XLA Ops:
  2.1 0.7 copy-start.8
  4.5 29.8 %copy-start.6 = (bf16[6,256,256]{2,1,0:T(8,128)(2,1)}, bf16[6,256,256]{2,1,0:T(8,128)(2,1)S(1)}, u32[]{:S(2)}) copy-start(bf16[6,256,256]{2,1,0:T(8,128)(2,1)S(1)} %convert_element_type.56) | copy-start | bytes 2359300
  25.3 9.0 copy-start.10
  245.3 3.9 copy-start.2
  266.2 2.0 copy-start
  640.1 3.9 copy-start.4
  687.1 5.5 copy-start.7
  687.1 5.5 copy-start.11
  687.1 187.6 %all-to-all-start.3 = ((bf16[2,512,1,4096]{3,0,2,1:T(2,128)(2,1)}), bf16[2,512,1,4096]{3,0,2,1:T(2,128)(2,1)}, u32[]{:S(2)}, u32[]{:S(2)}) async-start(bf16[2,512,1,4096]{3,0,2,1:T(2,128)(2,1)} %copy.129), calls=%async_computation.3 | async-start | bytes 16777216 | tf_op jit(solution)/shard_map/all_to_all | solution.py:64
  943.2 12.0 copy-start.9
  1199.1 3.9 copy-start.3
  1219.9 2.0 copy-start.1
  1581.3 3.9 copy-start.5
